TPU v7x, 32 devices: a whole 2x2x4 slice. The times are simulated.
32 devices in a mesh: tm: 8 (over z, y), row: 4 (over x, core).
Axes of the slice: x: 2, y: 2, z: 4, core: 2. Of those that a mesh axis runs over, the one named last changes fastest.
Arguments:
- lower: bfloat16 [16, 1024, 1024], P('tm', 'row'), may hold values from -0.1875 to 0.1875
- upper: bfloat16 [16, 1024, 1024], P('tm', 'row'), may hold values from -0.1875 to 0.1875
- shift_diag: float32 [16, 1024], P('tm', 'row'), may hold values from -0.5 to 0.5
- rhs: float32 [16, 1024, 128], P('tm', 'row'), may hold values from -6 to 6
Outputs:
- lower_two: bfloat16 [16, 1024, 1024], P('tm', 'row')
- upper_two: bfloat16 [16, 1024, 1024], P('tm', 'row')
- excess_two: bfloat16 [16, 1024, 1024], P('tm', 'row')
- rhs_two: float32 [16, 1024, 128], P('tm', 'row')
All inputs are finite; a program needn't handle non-finite values.
Results may differ from a plain program's by a relative error of at most 0.0083.
Values may be sent and summed in bfloat16 or wider, within the bound.
No kernel may reach another device: no remote copies, remote signals or barrier semaphores. Data moves between devices by JAX's collectives and lax.ppermute only.
A program may use at most 128 MiB of HBM per device.

v0:
```python
import jax
import jax.numpy as jnp
from jax import lax
from jax.sharding import PartitionSpec as P


def from_behind(array, axis, by):
    count = lax.axis_size(axis)
    pairs = [(i, i + by) for i in range(count) if 0 <= i + by < count]
    return lax.ppermute(array, axis, pairs)


def stacked(left_blocks, right_blocks):
    return jnp.einsum("bij,bjk->bik", left_blocks, right_blocks, preferred_element_type=jnp.float32)


def neighbour_terms(lower_rows, upper_rows, full_panel, distance):
    below_in = from_behind(full_panel[-distance:], "tm", 1)
    above_in = from_behind(full_panel[:distance], "tm", -1)
    below_panel = jnp.concatenate([below_in, full_panel[:-distance]], axis=0)
    above_panel = jnp.concatenate([full_panel[distance:], above_in], axis=0)
    return (stacked(lower_rows, below_panel), stacked(upper_rows, above_panel))


def apply_terms(below_term, above_term, excess_rows, rhs_rows, states):
    lower_new = (-below_term[:, :, :states]).astype(jnp.bfloat16)
    upper_new = (-above_term[:, :, states : 2 * states]).astype(jnp.bfloat16)
    excess_new = (
        excess_rows - below_term[:, :, states : 2 * states] - above_term[:, :, :states]
    ).astype(jnp.bfloat16)
    rhs_new = rhs_rows - below_term[:, :, 2 * states :] - above_term[:, :, 2 * states :]
    return (lower_new, upper_new, excess_new, rhs_new)


def shards(lower, upper, shift_diag, rhs):
    groups = lower.shape[0]
    height = lower.shape[1]
    states = lower.shape[2]
    offset = lax.axis_index("row") * height
    columns = lax.broadcasted_iota(jnp.int32, (groups, height, states), 2)
    row_pos = lax.broadcasted_iota(jnp.int32, (groups, height, states), 1) + offset
    excess_zero = jnp.where(columns == row_pos, shift_diag[:, :, None], 0.0)
    scaling = 1.0 - shift_diag
    panel_one = (
        scaling[:, :, None]
        * jnp.concatenate([lower.astype(jnp.float32), upper.astype(jnp.float32), rhs], axis=2)
    ).astype(jnp.bfloat16)
    full_one = lax.all_gather(panel_one, "row", axis=1, tiled=True)
    below_one, above_one = neighbour_terms(lower, upper, full_one, 1)
    lower_one, upper_one, excess_one, rhs_one = apply_terms(
        below_one, above_one, excess_zero, rhs, states
    )
    rhs_short = rhs_one.astype(jnp.bfloat16)
    own_rows = jnp.concatenate([lower_one, upper_one, rhs_short], axis=2)
    product = stacked(excess_one, lax.all_gather(own_rows, "row", axis=1, tiled=True))
    panel_two = (own_rows.astype(jnp.float32) - product).astype(jnp.bfloat16)
    full_two = lax.all_gather(panel_two, "row", axis=1, tiled=True)
    below_two, above_two = neighbour_terms(lower_one, upper_one, full_two, 2)
    return apply_terms(below_two, above_two, excess_one.astype(jnp.float32), rhs_one, states)


def solution(mesh):
    return jax.shard_map(
        shards,
        mesh=mesh,
        in_specs=(P("tm", "row", None), P("tm", "row", None), P("tm", "row"), P("tm", "row", None)),
        out_specs=(
            P("tm", "row", None),
            P("tm", "row", None),
            P("tm", "row", None),
            P("tm", "row", None),
        ),
        check_vma=False,
    )
```

profile of v0, /device:TPU:8, one launch (start us, length us, event | category | flops | bytes accessed | tf_op | source)
XLA Modules:
  0.0 850.0 jit_solution(13677663556818642498)
XLA Ops:
  7.9 1.1 copy.10
  9.0 1.5 copy.8
  10.6 1.5 copy.9
  12.3 1.7 fusion.15
  14.1 63.7 %all-gather.4.cloned.1.call-done = bf16[2,1024,2176]{1,2,0:T(8,128)(2,1)} async-done(((bf16[2,256,2176]{1,2,0:T(8,128)(2,1)}), bf16[2,1024,2176]{1,2,0:T(8,128)(2,1)}) %all-gather.4.cloned.1.call-update) | async-done | bytes 8912912 | tf_op jit(solution)/shard_map/all_gather | solution.py:48
  77.8 8.2 fusion.24
  86.0 3.4 collective-permute-start
  89.3 3.4 collective-permute-start.1
  92.7 188.3 %collective-permute-done = bf16[1,1024,2176]{1,2,0:T(8,128)(2,1)} collective-permute-done((bf16[1,1024,2176]{1,2,0:T(8,128)(2,1)}, bf16[1,1024,2176]{1,2,0:T(8,128)(2,1)}, u32[]{:S(2)}, u32[]{:S(2)}) %collective-permute-start) | collective-permute-done | bytes 4456480 | tf_op jit(solution)/shard_map/ppermute | solution.py:10
  281.0 5.1 fusion.11
  286.1 6.7 fusion.8
  292.9 0.9 fusion.18
  293.8 1.1 copy-done.2
  294.9 1.6 pad_maximum_fusion
  296.6 62.6 %all-gather.6.cloned.1.call-done = bf16[2,1024,2176]{1,2,0:T(8,128)(2,1)} async-done(((bf16[2,256,2176]{1,2,0:T(8,128)(2,1)}), bf16[2,1024,2176]{1,2,0:T(8,128)(2,1)}) %all-gather.6.cloned.1.call-update) | async-done | bytes 8912912 | tf_op jit(solution)/shard_map/all_gather | solution.py:55
  359.2 7.4 fusion.14
  366.6 62.6 %all-gather.8.cloned.1.call-done = bf16[2,1024,2176]{1,2,0:T(8,128)(2,1)} async-done(((bf16[2,256,2176]{1,2,0:T(8,128)(2,1)}), bf16[2,1024,2176]{1,2,0:T(8,128)(2,1)}) %all-gather.8.cloned.1.call-update) | async-done | bytes 8912912 | tf_op jit(solution)/shard_map/all_gather | solution.py:57
  429.2 3.3 collective-permute-start.3
  432.6 2.7 collective-permute-start.2
  435.3 380.9 %collective-permute-done.3 = bf16[2,1024,2176]{1,2,0:T(8,128)(2,1)S(1)} collective-permute-done((bf16[2,1024,2176]{1,2,0:T(8,128)(2,1)}, bf16[2,1024,2176]{1,2,0:T(8,128)(2,1)S(1)}, u32[]{:S(2)}, u32[]{:S(2)}) %collective-permute-start.3) | collective-permute-done | bytes 8912928 | tf_op jit(solution)/shard_map/ppermute | solution.py:10
  816.2 3.2 fusion.28
  819.4 1.6 fusion.26
  821.0 5.6 fusion.27
  827.4 2.0 fusion.25
  829.4 1.8 copy.33
  831.2 0.8 copy.35
  832.0 3.0 copy.32
  835.0 3.0 subtract_convert_fusion
  838.0 2.3 copy.23
  840.3 1.1 copy.34
  841.4 1.2 subtract_subtract_fusion
  842.6 0.8 copy.24
  (33 shorter events, 2.0 us)
Async XLA Ops:
  7.2 70.6 %all-gather.4.cloned.1.call-start = ((), (), s32[]{:S(2)}) async-start(), calls=%async_computation | async-start | bytes 11141120 | tf_op jit(solution)/shard_map/all_gather | solution.py:48
  14.0 267.0 %copy-start.6 = (bf16[2,256,1024]{2,1,0:T(8,128)(2,1)S(1)}, bf16[2,256,1024]{2,1,0:T(8,128)(2,1)}, u32[]{:S(2)}) copy-start(bf16[2,256,1024]{2,1,0:T(8,128)(2,1)} %param.4) | copy-start | bytes 3145732
  14.0 345.2 %all-gather.6.cloned.1.call-start = ((), (), s32[]{:S(2)}) async-start(), calls=%async_computation.1 | async-start | bytes 11141120 | tf_op jit(solution)/shard_map/all_gather | solution.py:55
  86.0 195.0 %collective-permute-start = (bf16[1,1024,2176]{1,2,0:T(8,128)(2,1)}, bf16[1,1024,2176]{1,2,0:T(8,128)(2,1)}, u32[]{:S(2)}, u32[]{:S(2)}) collective-permute-start(bf16[1,1024,2176]{1,2,0:T(8,128)(2,1)} %get-tuple-element.8), channel_id=1, source_target_pairs={{0,4},{4,8},{8,12},{12,16},{16,20},{20,24},{24,28},{1,5},{5,9},{9,... | collective-permute-start | bytes 13369352 | tf_op jit(solution)/shard_map/ppermute | solution.py:10
  89.3 196.8 %collective-permute-start.1 = (bf16[1,1024,2176]{1,2,0:T(8,128)(2,1)}, bf16[1,1024,2176]{1,2,0:T(8,128)(2,1)}, u32[]{:S(2)}, u32[]{:S(2)}) collective-permute-start(bf16[1,1024,2176]{1,2,0:T(8,128)(2,1)} %get-tuple-element.9), channel_id=1, source_target_pairs={{4,0},{8,4},{12,8},{16,12},{20,16},{24,20},{28,24},{5,1},{9,5},{13... | collective-permute-start | bytes 13369352 | tf_op jit(solution)/shard_map/ppermute | solution.py:10
  92.7 193.4 %copy-start.7 = (bf16[2,256,1024]{2,1,0:T(8,128)(2,1)S(1)}, bf16[2,256,1024]{2,1,0:T(8,128)(2,1)}, u32[]{:S(2)}) copy-start(bf16[2,256,1024]{2,1,0:T(8,128)(2,1)} %param.5) | copy-start | bytes 3145732
  286.1 6.8 copy-start.1
  286.1 6.8 copy-start.8
  292.8 2.1 copy-start.2
  294.9 71.7 %copy-start.4 = (bf16[2,256,1024]{1,2,0:T(8,128)(2,1)}, bf16[2,256,1024]{1,2,0:T(8,128)(2,1)S(1)}, u32[]{:S(2)}) copy-start(bf16[2,256,1024]{1,2,0:T(8,128)(2,1)S(1)} %get-tuple-element.14) | copy-start | bytes 3145732
  296.5 132.7 %all-gather.8.cloned.1.call-start = ((), (), s32[]{:S(2)}) async-start(), calls=%async_computation.2 | async-start | bytes 11141120 | tf_op jit(solution)/shard_map/all_gather | solution.py:57
  429.2 386.9 %collective-permute-start.3 = (bf16[2,1024,2176]{1,2,0:T(8,128)(2,1)}, bf16[2,1024,2176]{1,2,0:T(8,128)(2,1)S(1)}, u32[]{:S(2)}, u32[]{:S(2)}) collective-permute-start(bf16[2,1024,2176]{1,2,0:T(8,128)(2,1)} %all-gather.8.cloned.1.call-done), channel_id=1, source_target_pairs={{4,0},{8,4},{12,8},{16,12},{20,16},{24,20},{28,24},{5,1},{9,5},{13... | collective-permute-start | bytes 26738696 | tf_op jit(solution)/shard_map/ppermute | solution.py:10
  432.6 388.4 %collective-permute-start.2 = (bf16[2,1024,2176]{1,2,0:T(8,128)(2,1)}, bf16[2,1024,2176]{1,2,0:T(8,128)(2,1)}, u32[]{:S(2)}, u32[]{:S(2)}) collective-permute-start(bf16[2,1024,2176]{1,2,0:T(8,128)(2,1)} %all-gather.8.cloned.1.call-done), channel_id=1, source_target_pairs={{0,4},{4,8},{8,12},{12,16},{16,20},{20,24},{24,28},{1,5},{5,9},{9,... | collective-permute-start | bytes 26738696 | tf_op jit(solution)/shard_map/ppermute | solution.py:10
  819.4 7.2 copy-start.3
  827.4 3.8 slice-start
  831.2 3.9 copy-start
  832.0 3.0 copy-start.5
Sparse Core Ops, SparseCore 0:
  14.2 63.5 all-gather.3
  296.6 62.5 all-gather.5
  366.7 62.4 all-gather.7
where the time goes:
time: 850 us
  waiting for transfers between devices  758 us (89%)
  matrix products  27.9 us (3%)
  local copies, waits for them, and re-layouts  23.9 us (3%)
  between operations  14 us (2%)
  other arithmetic  13.1 us (2%)
  starting transfers between devices  12.9 us (2%)
    ppermute x4, waiting for transfers between devices, from_behind(): return lax.ppermute(array, axis, pairs)  569 us
    all_gather x1, waiting for transfers between devices, shards(): full_one = lax.all_gather(panel_one, 'row', axis=1, tiled=True)  63.7 us
    all_gather x1, waiting for transfers between devices, shards(): lax.all_gather(own_rows, 'row', axis=1, tiled=True)  62.6 us
    all_gather x1, waiting for transfers between devices, shards(): full_two = lax.all_gather(panel_two, 'row', axis=1, tiled=True)  62.6 us
    dot_general x5, matrix products, stacked(): jnp.einsum('bij,bjk->bik', left_blocks, right_blocks, preferred_element_t...  27.9 us
  transfers between devices with their start and end apart: 7, of which 5 were waited for; matrix products, arithmetic and copies ran while one was open for 1% of the time, Pallas kernels for 0%

commit v1 on v0

--- a/solution.py
+++ b/solution.py
@@ -2,6 +2,24 @@
 import jax.numpy as jnp
 from jax import lax
 from jax.sharding import PartitionSpec as P
+
+
+def match_entries(q_in, array_axis):
+    reached = list(q_in.shape[1:])
+    reached[array_axis] *= q_in.shape[0]
+    return jnp.moveaxis(q_in, 0, array_axis).reshape(reached)
+
+
+def _tell_turns(local_values, bus_axis):
+    n_all = lax.psum(1, bus_axis)
+    found_now = local_values[None]
+    for c in range(n_all.bit_length() - 1):
+        after = 1 << c
+        u1 = lax.ppermute(found_now, bus_axis, list(map(lambda no: (no, no ^ after), range(n_all))))
+        clean = jnp.stack([found_now, u1])
+        p_next = lax.axis_index(bus_axis) >> c & 1
+        found_now = jnp.where(p_next == 0, clean, clean[::-1]).reshape(-1, *local_values.shape)
+    return found_now
 
 
 def from_behind(array, axis, by):
@@ -54,7 +72,8 @@
     own_rows = jnp.concatenate([lower_one, upper_one, rhs_short], axis=2)
     product = stacked(excess_one, lax.all_gather(own_rows, "row", axis=1, tiled=True))
     panel_two = (own_rows.astype(jnp.float32) - product).astype(jnp.bfloat16)
-    full_two = lax.all_gather(panel_two, "row", axis=1, tiled=True)
+    prior = _tell_turns(panel_two, "row")
+    full_two = match_entries(prior, 1)
     below_two, above_two = neighbour_terms(lower_one, upper_one, full_two, 2)
     return apply_terms(below_two, above_two, excess_one.astype(jnp.float32), rhs_one, states)
 

time: 850 us -> 925 us (1.088)
  waiting for transfers between devices: 758 us -> 797 us
  other arithmetic: 13.1 us -> 40.2 us
  local copies, waits for them, and re-layouts: 23.9 us -> 34 us
    ppermute x0 -> x2, waiting for transfers between devices: none -> 103 us  [_tell_turns(): lax.ppermute(found_now, bus_axis, list(map(lambda no: (no, no ^ after), r...]
    all_gather x1 -> x0, waiting for transfers between devices: 62.6 us -> none  [shards(): full_two = lax.all_gather(panel_two, 'row', axis=1, tiled=True)]
    another operation x0 -> x3, other arithmetic: none -> 15.1 us  [_tell_turns(): clean = jnp.stack([found_now, u1])]
    transpose x0 -> x1, local copies, waits for them, and re-layouts: none -> 11.7 us  [match_entries(): return jnp.moveaxis(q_in, 0, array_axis).reshape(reached)]
    select_n x0 -> x1, other arithmetic: none -> 11.7 us  [_tell_turns(): jnp.where(p_next == 0, clean, clean[::-1]).reshape(-1, *local_values.shape)]
  transfers between devices with their start and end apart: 7 -> 8, of which waited for: 5 -> 6; matrix products, arithmetic and copies ran while one was open for 1% -> 1% of each run, Pallas kernels for 0% -> 0%
where the time goes in v1:
time: 925 us; the launch traced here: 924 us
  waiting for transfers between devices  797 us (86%)
  other arithmetic  40.2 us (4%)
  local copies, waits for them, and re-layouts  34 us (4%)
  matrix products  24.7 us (3%)
  between operations  14.3 us (2%)
  starting transfers between devices  13.9 us (2%)
    ppermute x4, waiting for transfers between devices, from_behind(): return lax.ppermute(array, axis, pairs)  568 us
    ppermute x2, waiting for transfers between devices, _tell_turns(): lax.ppermute(found_now, bus_axis, list(map(lambda no: (no, no ^ after), r...  103 us
    all_gather x1, waiting for transfers between devices, shards(): full_one = lax.all_gather(panel_one, 'row', axis=1, tiled=True)  63.7 us
    all_gather x1, waiting for transfers between devices, shards(): lax.all_gather(own_rows, 'row', axis=1, tiled=True)  62.7 us
    dot_general x5, matrix products, stacked(): jnp.einsum('bij,bjk->bik', left_blocks, right_blocks, preferred_element_t...  24.7 us
  transfers between devices with their start and end apart: 8, of which 6 were waited for; matrix products, arithmetic and copies ran while one was open for 1% of the time, Pallas kernels for 0%

profile of v1, /device:TPU:8, one launch (start us, length us, event | category | flops | bytes accessed | tf_op | source)
XLA Modules:
  0.0 924.2 jit_solution(10140587654727182487)
XLA Ops:
  9.0 1.5 copy.8
  10.6 1.5 copy.9
  12.3 1.7 fusion.15
  14.1 63.7 %all-gather.3.cloned.1.call-done = bf16[2,1024,2176]{1,2,0:T(8,128)(2,1)} async-done(((bf16[2,256,2176]{1,2,0:T(8,128)(2,1)}), bf16[2,1024,2176]{1,2,0:T(8,128)(2,1)}) %all-gather.3.cloned.1.call-update) | async-done | bytes 8912912 | tf_op jit(solution)/shard_map/all_gather | solution.py:66
  77.8 8.2 fusion.26
  86.0 3.4 collective-permute-start
  89.3 3.5 collective-permute-start.1
  92.9 188.1 %collective-permute-done = bf16[1,1024,2176]{1,2,0:T(8,128)(2,1)} collective-permute-done((bf16[1,1024,2176]{1,2,0:T(8,128)(2,1)}, bf16[1,1024,2176]{1,2,0:T(8,128)(2,1)}, u32[]{:S(2)}, u32[]{:S(2)}) %collective-permute-start) | collective-permute-done | bytes 4456480 | tf_op jit(solution)/shard_map/ppermute | solution.py:28
  281.0 5.1 fusion.11
  286.1 6.7 fusion.8
  294.9 1.6 pad_maximum_fusion.2
  296.5 62.7 %all-gather.5.cloned.1.call-done = bf16[2,1024,2176]{1,2,0:T(8,128)(2,1)} async-done(((bf16[2,256,2176]{1,2,0:T(8,128)(2,1)}), bf16[2,1024,2176]{1,2,0:T(8,128)(2,1)}) %all-gather.5.cloned.1.call-update) | async-done | bytes 8912912 | tf_op jit(solution)/shard_map/all_gather | solution.py:73
  359.2 7.4 fusion.14
  366.8 4.4 collective-permute-done.2
  371.3 2.7 pad_maximum_fusion.1
  374.0 4.5 fusion.17
  379.1 98.1 %collective-permute-done.3 = bf16[2,2,256,2176]{2,3,1,0:T(8,128)(2,1)} collective-permute-done((bf16[2,2,256,2176]{2,3,1,0:T(8,128)(2,1)}, bf16[2,2,256,2176]{2,3,1,0:T(8,128)(2,1)}, u32[]{:S(2)}, u32[]{:S(2)}) %collective-permute-start.3) | collective-permute-done | bytes 4456480 | tf_op jit(solution)/shard_map/ppermute | solution.py:18
  477.2 7.9 pad_maximum_fusion
  485.1 11.7 %reverse_select_fusion = bf16[2,2,2,256,2176]{3,4,2,1,0:T(8,128)(2,1)} fusion(bf16[2,2,2,256,2176]{3,4,2,1,0:T(8,128)(2,1)} %pad_maximum_fusion, pred[]{:T(512)S(6)} %eq.9), kind=kLoop, calls=%fused_computation | loop fusion | flops 4456448 | bytes 17825792 | tf_op jit(solution)/shard_map/jit(_where)/select_n | solution.py:21
  496.8 11.7 %copy.15 = bf16[2,4,256,2176]{3,2,1,0:T(8,128)(2,1)} copy(bf16[2,4,256,2176]{2,3,0,1:T(8,128)(2,1)} %bitcast.24) | data formatting | bytes 17825792 | tf_op jit(solution)/shard_map/transpose | solution.py:10
  508.5 3.3 collective-permute-start.5
  511.8 2.7 collective-permute-start.4
  514.5 380.1 %collective-permute-done.5 = bf16[2,1024,2176]{2,1,0:T(8,128)(2,1)S(1)} collective-permute-done((bf16[2,1024,2176]{2,1,0:T(8,128)(2,1)}, bf16[2,1024,2176]{2,1,0:T(8,128)(2,1)S(1)}, u32[]{:S(2)}, u32[]{:S(2)}) %collective-permute-start.5) | collective-permute-done | bytes 8912928 | tf_op jit(solution)/shard_map/ppermute | solution.py:28
  894.6 2.8 fusion.30
  897.4 1.6 fusion.28
  899.1 2.8 fusion.29
  902.6 2.0 fusion.27
  904.7 1.8 copy.30
  906.6 3.0 copy.29
  909.7 3.3 subtract_convert_fusion
  913.0 2.3 copy.22
  915.4 1.1 subtract_subtract_fusion
  (39 shorter events, 6.9 us)
Async XLA Ops:
  7.2 70.6 %all-gather.3.cloned.1.call-start = ((), (), s32[]{:S(2)}) async-start(), calls=%async_computation | async-start | bytes 11141120 | tf_op jit(solution)/shard_map/all_gather | solution.py:66
  14.0 267.0 %copy-start.5 = (bf16[2,256,1024]{2,1,0:T(8,128)(2,1)S(1)}, bf16[2,256,1024]{2,1,0:T(8,128)(2,1)}, u32[]{:S(2)}) copy-start(bf16[2,256,1024]{2,1,0:T(8,128)(2,1)} %param.4) | copy-start | bytes 3145732
  14.0 345.2 %all-gather.5.cloned.1.call-start = ((), (), s32[]{:S(2)}) async-start(), calls=%async_computation.1 | async-start | bytes 11141120 | tf_op jit(solution)/shard_map/all_gather | solution.py:73
  86.0 195.0 %collective-permute-start = (bf16[1,1024,2176]{1,2,0:T(8,128)(2,1)}, bf16[1,1024,2176]{1,2,0:T(8,128)(2,1)}, u32[]{:S(2)}, u32[]{:S(2)}) collective-permute-start(bf16[1,1024,2176]{1,2,0:T(8,128)(2,1)} %get-tuple-element.8), channel_id=1, source_target_pairs={{0,4},{4,8},{8,12},{12,16},{16,20},{20,24},{24,28},{1,5},{5,9},{9,... | collective-permute-start | bytes 13369352 | tf_op jit(solution)/shard_map/ppermute | solution.py:28
  89.3 196.8 %collective-permute-start.1 = (bf16[1,1024,2176]{1,2,0:T(8,128)(2,1)}, bf16[1,1024,2176]{1,2,0:T(8,128)(2,1)}, u32[]{:S(2)}, u32[]{:S(2)}) collective-permute-start(bf16[1,1024,2176]{1,2,0:T(8,128)(2,1)} %get-tuple-element.9), channel_id=1, source_target_pairs={{4,0},{8,4},{12,8},{16,12},{20,16},{24,20},{28,24},{5,1},{9,5},{13... | collective-permute-start | bytes 13369352 | tf_op jit(solution)/shard_map/ppermute | solution.py:28
  92.9 193.2 %copy-start.6 = (bf16[2,256,1024]{2,1,0:T(8,128)(2,1)S(1)}, bf16[2,256,1024]{2,1,0:T(8,128)(2,1)}, u32[]{:S(2)}) copy-start(bf16[2,256,1024]{2,1,0:T(8,128)(2,1)} %param.5) | copy-start | bytes 3145732
  286.1 6.8 copy-start.2
  286.1 6.8 copy-start.8
  292.8 2.1 copy-start.3
  294.9 71.7 %copy-start.4 = (bf16[2,256,1024]{1,2,0:T(8,128)(2,1)}, bf16[2,256,1024]{1,2,0:T(8,128)(2,1)S(1)}, u32[]{:S(2)}) copy-start(bf16[2,256,1024]{1,2,0:T(8,128)(2,1)S(1)} %get-tuple-element.16) | copy-start | bytes 3145732
  366.6 4.7 collective-permute-start.2
  378.5 98.7 %collective-permute-start.3 = (bf16[2,2,256,2176]{2,3,1,0:T(8,128)(2,1)}, bf16[2,2,256,2176]{2,3,1,0:T(8,128)(2,1)}, u32[]{:S(2)}, u32[]{:S(2)}) collective-permute-start(bf16[2,2,256,2176]{2,3,1,0:T(8,128)(2,1)} %get-tuple-element.15), channel_id=1, source_target_pairs={{0,2},{1,3},{2,0},{3,1},{4,6},{5,7},{6,4},{7,5},{8,10},{9,11},{10,... | collective-permute-start | bytes 13369352 | tf_op jit(solution)/shard_map/ppermute | solution.py:18
  508.5 386.1 %collective-permute-start.5 = (bf16[2,1024,2176]{2,1,0:T(8,128)(2,1)}, bf16[2,1024,2176]{2,1,0:T(8,128)(2,1)S(1)}, u32[]{:S(2)}, u32[]{:S(2)}) collective-permute-start(bf16[2,1024,2176]{2,1,0:T(8,128)(2,1)} %bitcast.25), channel_id=1, source_target_pairs={{4,0},{8,4},{12,8},{16,12},{20,16},{24,20},{28,24},{5,1},{9,5},{13... | collective-permute-start | bytes 26738696 | tf_op jit(solution)/shard_map/ppermute | solution.py:28
  511.8 387.3 %collective-permute-start.4 = (bf16[2,1024,2176]{2,1,0:T(8,128)(2,1)}, bf16[2,1024,2176]{2,1,0:T(8,128)(2,1)S(1)}, u32[]{:S(2)}, u32[]{:S(2)}) collective-permute-start(bf16[2,1024,2176]{2,1,0:T(8,128)(2,1)} %bitcast.26), channel_id=1, source_target_pairs={{0,4},{4,8},{8,12},{12,16},{16,20},{20,24},{24,28},{1,5},{5,9},{9,... | collective-permute-start | bytes 26738696 | tf_op jit(solution)/shard_map/ppermute | solution.py:28
  897.4 4.5 copy-start
  902.6 3.8 slice-start
  906.5 3.2 copy-start.1
  909.7 5.6 copy-start.7
Sparse Core Ops, SparseCore 0:
  14.2 63.5 all-gather.2
  296.6 62.5 all-gather.4
